TPU v7x, 128 devices: a whole 4x4x4 slice. The times are simulated.
128 devices in a mesh: group: 4 (over x), tile: 32 (over z, y, core).
Axes of the slice: x: 4, y: 4, z: 4, core: 2. Of those that a mesh axis runs over, the one named last changes fastest.
Arguments:
- frames: bfloat16 [12, 8, 128, 96, 256], P('group', None, 'tile'), may hold values from -6 to 6
- packing: int32 [12, 4], replicated, as said below
- w_space: bfloat16 [3, 3, 96, 96], replicated, may hold values from -0.21875 to 0.21875
- w_time: bfloat16 [3, 96, 96], replicated, may hold values from -0.375 to 0.375
- gain_one: float32 [96], replicated, may hold values from 0.1 to 1.9
- gain_two: float32 [96], replicated, may hold values from 0.1 to 1.9
Outputs:
- output: bfloat16 [12, 8, 128, 96, 256], P('group', None, 'tile')
Inputs may be any that keep to these rules, and one draw needn't show every extreme that they name: `packing`: column 0 is 1 where the slot's span continues a clip and 0 for a clip's first span, whose other source fields are not read. `packing`: a span with a successor has 8 valid frames, so every preceding span is full; the slots of one device have their preceding spans on distinct devices.
All inputs are finite; a program needn't handle non-finite values.
Results may differ from a plain program's by a relative error of at most 0.004.
Values may be sent and summed in bfloat16 or wider, within the bound.
No kernel may reach another device: no remote copies, remote signals or barrier semaphores. Data moves between devices by JAX's collectives and lax.ppermute only.
A program may use at most 192 MiB of HBM per device.

v0:
```python
import jax
import jax.numpy as jnp
from jax import lax
from jax.sharding import PartitionSpec as P


def extended_2(block, sides, width):
    for axis, dim in sides:
        count = lax.axis_size(axis)
        forward = [(i, i + 1) for i in range(count - 1)]
        backward = [(target, source) for source, target in forward]
        low = lax.ppermute(
            lax.slice_in_dim(block, block.shape[dim] - width, None, axis=dim), axis, forward
        )
        high = lax.ppermute(lax.slice_in_dim(block, 0, width, axis=dim), axis, backward)
        block = jnp.concatenate([low, block, high], axis=dim)
    return block


def norm_act(values, gain_vec):
    meansq = jnp.mean(values * values, axis=-2, keepdims=True)
    return jax.nn.silu(values * lax.rsqrt(meansq + 1e-06) * gain_vec[:, None])


def body(frames, packing, w_space, w_time, gain_one, gain_two):
    slot_count, frame_count, row_count, chan_count, col_count = frames.shape
    own_index = lax.axis_index("group")
    mine = lax.dynamic_slice_in_dim(packing, own_index * slot_count, slot_count, 0)
    hidden = norm_act(frames.astype(jnp.float32), gain_one).astype(jnp.bfloat16)
    rimmed = extended_2(hidden, (("tile", 2),), 1)
    padded = jnp.pad(rimmed, ((0, 0), (0, 0), (0, 0), (0, 0), (1, 1)))
    summed = jnp.zeros(frames.shape, jnp.float32)
    for tap_row in range(3):
        for tap_col in range(3):
            window = padded[:, :, tap_row : tap_row + row_count, :, tap_col : tap_col + col_count]
            summed = summed + jnp.einsum(
                "oi,nfyix->nfyox",
                w_space[tap_row, tap_col],
                window,
                preferred_element_type=jnp.float32,
            )
    act = norm_act(summed, gain_two).astype(jnp.bfloat16)
    tails = act[:, frame_count - 2 :]
    has_prev = mine[:, 0] > 0
    wanted = mine[:, 2] * slot_count + mine[:, 3]
    piece = lax.all_gather(tails, "group", axis=0, tiled=True)
    global_ids = jnp.arange(piece.shape[0], dtype=jnp.int32)
    select = ((wanted[:, None] == global_ids[None, :]) & has_prev[:, None]).astype(jnp.bfloat16)
    picked = jnp.einsum("sk,kfyix->sfyix", select, piece, preferred_element_type=jnp.float32)
    cache = picked.astype(jnp.bfloat16)
    extended = jnp.concatenate([cache, act], axis=1)
    temporal = jnp.zeros(frames.shape, jnp.float32)
    for tap in range(3):
        temporal = temporal + jnp.einsum(
            "oi,nfyix->nfyox",
            w_time[tap],
            extended[:, tap : tap + frame_count],
            preferred_element_type=jnp.float32,
        )
    keep = jnp.arange(frame_count, dtype=jnp.int32)[None, :] < mine[:, 1][:, None]
    result = jnp.where(keep[:, :, None, None, None], frames.astype(jnp.float32) + temporal, 0.0)
    return result.astype(jnp.bfloat16)


def solution(mesh):
    in_specs = (P("group", None, "tile", None, None), P(), P(), P(), P(), P())
    out_specs = P("group", None, "tile", None, None)
    return jax.shard_map(body, mesh=mesh, in_specs=in_specs, out_specs=out_specs, check_vma=False)
```

profile of v0, /device:TPU:1, one launch (start us, length us, event | category | flops | bytes accessed | tf_op | source)
XLA Modules:
  0.0 205.3 jit_solution(2057114716746689768)
XLA Ops:
  6.5 3.9 %fusion.6 = f32[3,8,4,256]{3,2,1,0:T(4,128)S(1)} fusion(bf16[3,8,4,96,256]{4,3,2,1,0:T(8,128)(2,1)} %param.6), kind=kLoop, calls=%fused_computation.11 | loop fusion | flops 7053312 | bytes 4816896 | tf_op jit(solution)/shard_map/reduce_sum | solution.py:21
  10.5 4.8 %fusion.13 = bf16[3,8,4,96,256]{4,3,2,1,0:T(8,128)(2,1)S(1)} fusion(bf16[3,8,4,96,256]{4,3,2,1,0:T(8,128)(2,1)} %param.6, f32[96]{0:T(128)} %param.10, f32[3,8,4,256]{3,2,1,0:T(4,128)S(1)} %add_rsqrt_fusion.1), kind=kLoop, calls=%fused_computation.18 | loop fusion | flops 18874368 | bytes 9535872 | tf_op jit(solution)/shard_map/convert_element_type | solution.py:29
  15.3 0.2 fusion.80
  15.5 4.6 %collective-permute-start = (bf16[3,8,1,96,256]{4,3,2,1,0:T(8,128)(2,1)S(1)}, bf16[3,8,1,96,256]{4,3,2,1,0:T(8,128)(2,1)S(1)}, u32[]{:S(2)}, u32[]{:S(2)}) collective-permute-start(bf16[3,8,1,96,256]{4,3,2,1,0:T(8,128)(2,1)S(1)} %get-tuple-element.5), channel_id=1, source_target_pairs={{0,1},{1,2},{2,3},{3,4},{4,5},{5,6},{6,7},{7,8},{8,9},{9,10},{10,1... | collective-permute-start | bytes 3538952 | tf_op jit(solution)/shard_map/ppermute | solution.py:12
  20.1 2.1 %collective-permute-start.1 = (bf16[3,8,1,96,256]{4,3,2,1,0:T(8,128)(2,1)S(1)}, bf16[3,8,1,96,256]{4,3,2,1,0:T(8,128)(2,1)S(1)}, u32[]{:S(2)}, u32[]{:S(2)}) collective-permute-start(bf16[3,8,1,96,256]{4,3,2,1,0:T(8,128)(2,1)S(1)} %get-tuple-element.6), channel_id=1, source_target_pairs={{1,0},{2,1},{3,2},{4,3},{5,4},{6,5},{7,6},{8,7},{9,8},{10,9},{11,1... | collective-permute-start | bytes 3538952 | tf_op jit(solution)/shard_map/ppermute | solution.py:15
  22.2 0.0 copy-done.3
  22.2 5.0 %fusion.53 = f32[3,8,4,256,96]{3,4,2,1,0:T(8,128)} fusion(bf16[3,8,4,96,256]{4,3,2,1,0:T(8,128)(2,1)S(1)} %fusion.13, bf16[3,3,96,96]{3,2,1,0:T(8,128)(2,1)S(1)} %copy-done.3), kind=kOutput, calls=%fused_computation.67 | convolution fusion | flops 452984832 | bytes 14180352 | tf_op jit(solution)/shard_map/oi,nfyix->nfyox/dot_general | solution.py:36
  27.3 6.0 %collective-permute-done = bf16[3,8,1,96,256]{4,3,2,1,0:T(8,128)(2,1)S(1)} collective-permute-done((bf16[3,8,1,96,256]{4,3,2,1,0:T(8,128)(2,1)S(1)}, bf16[3,8,1,96,256]{4,3,2,1,0:T(8,128)(2,1)S(1)}, u32[]{:S(2)}, u32[]{:S(2)}) %collective-permute-start) | collective-permute-done | bytes 1179680 | tf_op jit(solution)/shard_map/ppermute | solution.py:12
  33.2 4.4 %collective-permute-done.1 = bf16[3,8,1,96,256]{4,3,2,1,0:T(8,128)(2,1)S(1)} collective-permute-done((bf16[3,8,1,96,256]{4,3,2,1,0:T(8,128)(2,1)S(1)}, bf16[3,8,1,96,256]{4,3,2,1,0:T(8,128)(2,1)S(1)}, u32[]{:S(2)}, u32[]{:S(2)}) %collective-permute-start.1) | collective-permute-done | bytes 1179680 | tf_op jit(solution)/shard_map/ppermute | solution.py:15
  37.6 7.1 %fusion.5 = bf16[3,8,6,96,258]{4,3,2,1,0:T(8,128)(2,1)S(1)} fusion(bf16[3,8,1,96,256]{4,3,2,1,0:T(8,128)(2,1)S(1)} %collective-permute-done.1, bf16[3,8,4,96,256]{4,3,2,1,0:T(8,128)(2,1)S(1)} %fusion.13, bf16[3,8,1,96,256]{4,3,2,1,0:T(8,128)(2,1)S(1)} %collective-permute-done), kind=kLoop, calls=%fused_computation.10 | loop fusion | flops 42799104 | bytes 14211072 | tf_op jit(solution)/shard_map/concatenate | solution.py:16
  44.7 5.5 %fusion.31 = f32[3,8,4,256,96]{3,4,2,1,0:T(8,128)} fusion(bf16[3,8,6,96,258]{4,3,2,1,0:T(8,128)(2,1)S(1)} %fusion.5, bf16[3,3,96,96]{3,2,1,0:T(8,128)(2,1)S(1)} %copy-done.3), kind=kOutput, calls=%fused_computation.43 | convolution fusion | flops 452984832 | bytes 14180352 | tf_op jit(solution)/shard_map/oi,nfyix->nfyox/dot_general | solution.py:36
  50.2 5.2 %fusion.33 = f32[3,8,4,256,96]{3,4,2,1,0:T(8,128)} fusion(bf16[3,8,6,96,258]{4,3,2,1,0:T(8,128)(2,1)S(1)} %fusion.5, bf16[3,3,96,96]{3,2,1,0:T(8,128)(2,1)S(1)} %copy-done.3), kind=kOutput, calls=%fused_computation.45 | convolution fusion | flops 452984832 | bytes 14180352 | tf_op jit(solution)/shard_map/oi,nfyix->nfyox/dot_general | solution.py:36
  55.3 5.1 %fusion.35 = f32[3,8,4,256,96]{3,4,2,1,0:T(8,128)} fusion(bf16[3,8,6,96,258]{4,3,2,1,0:T(8,128)(2,1)S(1)} %fusion.5, bf16[3,3,96,96]{3,2,1,0:T(8,128)(2,1)S(1)} %copy-done.3), kind=kOutput, calls=%fused_computation.47 | convolution fusion | flops 452984832 | bytes 14180352 | tf_op jit(solution)/shard_map/oi,nfyix->nfyox/dot_general | solution.py:36
  60.4 5.1 %fusion.37 = f32[3,8,4,256,96]{3,4,2,1,0:T(8,128)} fusion(bf16[3,8,6,96,258]{4,3,2,1,0:T(8,128)(2,1)S(1)} %fusion.5, bf16[3,3,96,96]{3,2,1,0:T(8,128)(2,1)S(1)} %copy-done.3), kind=kOutput, calls=%fused_computation.49 | convolution fusion | flops 452984832 | bytes 14180352 | tf_op jit(solution)/shard_map/oi,nfyix->nfyox/dot_general | solution.py:36
  65.5 4.9 %fusion.41 = f32[3,8,4,256,96]{3,4,2,1,0:T(8,128)} fusion(bf16[3,8,6,96,258]{4,3,2,1,0:T(8,128)(2,1)S(1)} %fusion.5, bf16[3,3,96,96]{3,2,1,0:T(8,128)(2,1)S(1)} %copy-done.3), kind=kOutput, calls=%fused_computation.54 | convolution fusion | flops 452984832 | bytes 14180352 | tf_op jit(solution)/shard_map/oi,nfyix->nfyox/dot_general | solution.py:36
  70.5 5.1 %fusion.29 = f32[3,8,4,256,96]{3,4,2,1,0:T(8,128)} fusion(bf16[3,8,1,96,256]{4,3,2,1,0:T(8,128)(2,1)S(1)} %collective-permute-done.1, bf16[3,8,4,96,256]{4,3,2,1,0:T(8,128)(2,1)S(1)} %fusion.13, bf16[3,3,96,96]{3,2,1,0:T(8,128)(2,1)S(1)} %copy-done.3), kind=kOutput, calls=%fused_computation.41 | convolution fusion | flops 462422016 | bytes 15360000 | tf_op jit(solution)/shard_map/oi,nfyix->nfyox/dot_general | solution.py:36
  75.6 4.4 %fusion.39 = f32[3,8,4,256,96]{3,4,2,1,0:T(8,128)} fusion(bf16[3,8,4,96,256]{4,3,2,1,0:T(8,128)(2,1)S(1)} %fusion.13, bf16[3,8,1,96,256]{4,3,2,1,0:T(8,128)(2,1)S(1)} %collective-permute-done, bf16[3,3,96,96]{3,2,1,0:T(8,128)(2,1)S(1)} %copy-done.3), kind=kOutput, calls=%fused_computation.52 | convolution fusion | flops 462422016 | bytes 15360000 | tf_op jit(solution)/shard_map/oi,nfyix->nfyox/dot_general | solution.py:36
  80.0 31.7 %multiply_reduce_fusion = (f32[3,8,4,256]{3,2,1,0:T(4,128)S(1)}, f32[3,8,4,256,96]{3,4,2,1,0:T(8,128)}) fusion(bf16[3,8,6,96,258]{4,3,2,1,0:T(8,128)(2,1)} %copy-done.1, bf16[3,3,96,96]{3,2,1,0:T(8,128)(2,1)S(1)} %copy-done.3, f32[3,8,4,256,96]{3,4,2,1,0:T(8,128)} %fusion.29, f32[3,8,4,256,96]{3,4,2,1,0:T(8,128)} %fusion.31, ...), kind=kOutput, calls=%fused_computation.26 | convolution fusion | flops 476553216 | bytes 89776128 | tf_op jit(solution)/shard_map/oi,nfyix->nfyox/dot_general | solution.py:36
  111.7 0.0 copy-start.4
  111.8 5.8 %fusion.19 = bf16[3,8,4,96,256]{4,3,2,1,0:T(8,128)(2,1)S(1)} fusion(f32[3,8,4,256,96]{3,4,2,1,0:T(8,128)} %get-tuple-element.10, f32[96]{0:T(128)S(1)} %copy-done.5, f32[3,8,4,256]{3,2,1,0:T(4,128)S(1)} %add_rsqrt_fusion), kind=kLoop, calls=%fused_computation.28 | loop fusion | flops 16515072 | bytes 14254464 | tf_op jit(solution)/shard_map/convert_element_type | solution.py:42
  117.6 0.0 copy-start.2
  117.6 2.2 %copy-done.2 = bf16[3,8,4,96,256]{4,3,2,1,0:T(8,128)(2,1)} copy-done((bf16[3,8,4,96,256]{4,3,2,1,0:T(8,128)(2,1)}, bf16[3,8,4,96,256]{4,3,2,1,0:T(8,128)(2,1)S(1)}, u32[]{:S(2)}) %copy-start.2) | copy-done | bytes 4718616
  119.7 1.1 slice.133
  120.8 0.0 all-gather.2.cloned.1.call-update
  120.9 0.1 constant_dynamic-slice_fusion
  121.0 0.1 iota_compare_fusion.3
  121.0 7.4 %fusion.45 = f32[3,8,4,256,96]{3,4,2,1,0:T(8,128)} fusion(bf16[3,8,4,96,256]{4,3,2,1,0:T(8,128)(2,1)} %copy-done.2, bf16[3,96,96]{2,1,0:T(8,128)(2,1)S(1)} %copy-done.4), kind=kOutput, calls=%fused_computation.59 | convolution fusion | flops 452984832 | bytes 14180352 | tf_op jit(solution)/shard_map/oi,nfyix->nfyox/dot_general | solution.py:54
  128.4 48.3 %all-gather.2.cloned.1.call-done = bf16[12,2,4,96,256]{4,3,2,1,0:T(8,128)(2,1)} async-done(((bf16[3,2,4,96,256]{4,3,2,1,0:T(8,128)(2,1)}), bf16[12,2,4,96,256]{4,3,2,1,0:T(8,128)(2,1)}) %all-gather.2.cloned.1.call-update) | async-done | bytes 4718608 | tf_op jit(solution)/shard_map/all_gather | solution.py:46
  176.7 5.4 %fusion.20 = bf16[3,2,4,96,256]{4,0,3,2,1:T(4,128)(2,1)S(1)} fusion(bf16[12,2,4,96,256]{4,3,2,1,0:T(8,128)(2,1)} %all-gather.2.cloned.1.call-done, s32[3]{0:T(128)S(1)} %get-tuple-element.8, pred[3]{0:T(512)(128)(4,1)S(1)} %compare_bitcast_fusion), kind=kOutput, calls=%fused_computation.29 | convolution fusion | flops 14155848 | bytes 5898255 | tf_op jit(solution)/shard_map/sk,kfyix->sfyix/dot_general | solution.py:49
  182.1 0.2 copy.27
  182.4 4.4 %fusion.23 = f32[3,8,4,256,96]{3,4,2,1,0:T(8,128)} fusion(bf16[3,2,4,96,256]{4,3,2,1,0:T(8,128)(2,1)S(1)} %copy.27, bf16[3,8,4,96,256]{4,3,2,1,0:T(8,128)(2,1)S(1)} %bitcast.115, bf16[3,96,96]{2,1,0:T(8,128)(2,1)S(1)} %copy-done.4), kind=kOutput, calls=%fused_computation.34 | convolution fusion | flops 462422016 | bytes 15360000 | tf_op jit(solution)/shard_map/oi,nfyix->nfyox/dot_general | solution.py:54
  186.8 11.7 %fusion.15 = bf16[3,8,4,96,256]{4,3,2,1,0:T(8,128)(2,1)} fusion(bf16[3,8,4,96,256]{4,3,2,1,0:T(8,128)(2,1)} %param.6, f32[3,8,4,256,96]{3,4,2,1,0:T(8,128)} %fusion.45, f32[3,8,4,256,96]{3,4,2,1,0:T(8,128)} %fusion.23, pred[3,8]{1,0:T(4,128)(4,1)S(1)} %iota_compare_fusion.3, bf16[3,8,4,96,256]{4,3,2,1,0:T(8,128)(2,1)S(1)} %bitcast.115, ...), kind=kOutput, calls=%fused_computation.20 | convolution fusion | flops 476577792 | bytes 34234880 | tf_op jit(solution)/shard_map/oi,nfyix->nfyox/dot_general | solution.py:54
  (18 shorter events, 0.1 us)
Async XLA Ops:
  6.5 114.3 %copy-start = (s32[12,4]{0,1:T(4,128)S(1)}, s32[12,4]{0,1:T(4,128)}, u32[]{:S(2)}) copy-start(s32[12,4]{0,1:T(4,128)} %param.7) | copy-start | bytes 580
  6.5 15.7 %copy-start.3 = (bf16[3,3,96,96]{3,2,1,0:T(8,128)(2,1)S(1)}, bf16[3,3,96,96]{3,2,1,0:T(8,128)(2,1)}, u32[]{:S(2)}) copy-start(bf16[3,3,96,96]{3,2,1,0:T(8,128)(2,1)} %param.8) | copy-start | bytes 497668
  6.5 170.2 %all-gather.2.cloned.1.call-start = ((), (), s32[]{:S(2)}) async-start(), calls=%async_computation | async-start | bytes 5898240 | tf_op jit(solution)/shard_map/all_gather | solution.py:46
  15.5 17.7 %collective-permute-start = (bf16[3,8,1,96,256]{4,3,2,1,0:T(8,128)(2,1)S(1)}, bf16[3,8,1,96,256]{4,3,2,1,0:T(8,128)(2,1)S(1)}, u32[]{:S(2)}, u32[]{:S(2)}) collective-permute-start(bf16[3,8,1,96,256]{4,3,2,1,0:T(8,128)(2,1)S(1)} %get-tuple-element.5), channel_id=1, source_target_pairs={{0,1},{1,2},{2,3},{3,4},{4,5},{5,6},{6,7},{7,8},{8,9},{9,10},{10,1... | collective-permute-start | bytes 3538952 | tf_op jit(solution)/shard_map/ppermute | solution.py:12
  20.1 17.5 %collective-permute-start.1 = (bf16[3,8,1,96,256]{4,3,2,1,0:T(8,128)(2,1)S(1)}, bf16[3,8,1,96,256]{4,3,2,1,0:T(8,128)(2,1)S(1)}, u32[]{:S(2)}, u32[]{:S(2)}) collective-permute-start(bf16[3,8,1,96,256]{4,3,2,1,0:T(8,128)(2,1)S(1)} %get-tuple-element.6), channel_id=1, source_target_pairs={{1,0},{2,1},{3,2},{4,3},{5,4},{6,5},{7,6},{8,7},{9,8},{10,9},{11,1... | collective-permute-start | bytes 3538952 | tf_op jit(solution)/shard_map/ppermute | solution.py:15
  44.7 20.8 %copy-start.1 = (bf16[3,8,6,96,258]{4,3,2,1,0:T(8,128)(2,1)}, bf16[3,8,6,96,258]{4,3,2,1,0:T(8,128)(2,1)S(1)}, u32[]{:S(2)}) copy-start(bf16[3,8,6,96,258]{4,3,2,1,0:T(8,128)(2,1)S(1)} %fusion.5) | copy-start | bytes 21399556
  80.0 31.8 %copy-start.5 = (f32[96]{0:T(128)S(1)}, f32[96]{0:T(128)}, u32[]{:S(2)}) copy-start(f32[96]{0:T(128)} %param.11) | copy-start | bytes 1156
  111.7 9.4 %copy-start.4 = (bf16[3,96,96]{2,1,0:T(8,128)(2,1)S(1)}, bf16[3,96,96]{2,1,0:T(8,128)(2,1)}, u32[]{:S(2)}) copy-start(bf16[3,96,96]{2,1,0:T(8,128)(2,1)} %param.9) | copy-start | bytes 165892
  117.6 2.2 %copy-start.2 = (bf16[3,8,4,96,256]{4,3,2,1,0:T(8,128)(2,1)}, bf16[3,8,4,96,256]{4,3,2,1,0:T(8,128)(2,1)S(1)}, u32[]{:S(2)}) copy-start(bf16[3,8,4,96,256]{4,3,2,1,0:T(8,128)(2,1)S(1)} %fusion.19) | copy-start | bytes 14155780
  128.4 53.9 %slice-start = ((s8[4718592]{0:T(1024)(128)(4,1)}), s8[524288]{0:T(1024)(128)(4,1)S(1)}, s32[]{:S(2)}) async-start(s8[4718592]{0:T(1024)(128)(4,1)} %bitcast.114), calls=%async_computation.1 | async-start | bytes 1048576
  176.7 5.6 %slice-start.1 = ((s8[4718592]{0:T(1024)(128)(4,1)}), s8[4194304]{0:T(1024)(128)(4,1)S(1)}, s32[]{:S(2)}) async-start(s8[4718592]{0:T(1024)(128)(4,1)} %bitcast.114), calls=%async_computation.2 | async-start | bytes 8388608
Sparse Core Ops, SparseCore 0:
  121.0 55.6 all-gather.1
where the time goes:
time: 205 us
  matrix products  101 us (49%)
  waiting for transfers between devices  58.7 us (29%)
  other arithmetic  21.8 us (11%)
  between operations  13.6 us (7%)
  starting transfers between devices  6.69 us (3%)
  local copies, waits for them, and re-layouts  3.75 us (2%)
    dot_general x9, matrix products, body(): jnp.einsum('oi,nfyix->nfyox', w_space[tap_row, tap_col], window, preferre...  72 us
    all_gather x1, waiting for transfers between devices, body(): piece = lax.all_gather(tails, 'group', axis=0, tiled=True)  48.3 us
    dot_general x3, matrix products, body(): jnp.einsum('oi,nfyix->nfyox', w_time[tap], extended[:, tap:tap + frame_co...  23.5 us
    concatenate x1, other arithmetic, extended_2(): block = jnp.concatenate([low, block, high], axis=dim)  7.08 us
    ppermute x1, waiting for transfers between devices, extended_2(): lax.ppermute(lax.slice_in_dim(block, block.shape[dim] - width, None, axis...  5.96 us
    convert_element_type x1, other arithmetic, body(): act = norm_act(summed, gain_two).astype(jnp.bfloat16)  5.78 us
    dot_general x1, matrix products, body(): jnp.einsum('sk,kfyix->sfyix', select, piece, preferred_element_type=jnp.f...  5.4 us
    convert_element_type x1, other arithmetic, body(): hidden = norm_act(frames.astype(jnp.float32), gain_one).astype(jnp.bfloat16)  4.83 us
  transfers between devices with their start and end apart: 3, of which 3 were waited for; matrix products, arithmetic and copies ran while one was open for 6% of the time, Pallas kernels for 0%

commit v1 on v0

v1 whole, which is shorter than its diff:
```python
import functools

import jax
import jax.numpy as jnp
from jax import lax
from jax.experimental import pallas as pl
from jax.experimental.pallas import tpu as pltpu
from jax.sharding import PartitionSpec as P

F32 = jnp.float32
BF16 = jnp.bfloat16
TAIL = 2


def silu_norm(values, half_gain):
    meansq = jnp.mean(values * values, axis=0, keepdims=True)
    half = values * lax.rsqrt(meansq + 1e-06) * half_gain
    return (half + half * jnp.tanh(half)).astype(BF16)


def put_row(scr, row, chan, hidden):
    cols = hidden.shape[1]
    lane = lax.broadcasted_iota(jnp.int32, hidden.shape, 1)
    zero = jnp.zeros_like(hidden)
    left = jnp.where(lane == 0, zero, pltpu.roll(hidden, 1, 1))
    right = jnp.where(lane == cols - 1, zero, pltpu.roll(hidden, cols - 1, 1))
    base = row * (3 * chan)
    if not isinstance(base, int):
        base = pl.multiple_of(base, 32)
    scr[pl.ds(base, chan), :] = left
    scr[pl.ds(base + chan, chan), :] = hidden
    scr[pl.ds(base + 2 * chan, chan), :] = right


def act_rows(rows, frame, pair, out, wcat, gain_one, gain_two, scr, odd):
    chan = gain_one.shape[0]
    half_one = gain_one[...]
    put_row(scr, (1 - odd) * (rows + 1), chan, silu_norm(pair(), half_one))
    put_row(scr, odd * (rows + 1), chan, silu_norm(out(), half_one))
    for y in range(rows):
        put_row(scr, y + 1, chan, silu_norm(frame(y), half_one))
    half_two = gain_two[...]
    result = []
    for y in range(rows):
        window = scr[y * 3 * chan : (y + 3) * 3 * chan, :]
        spatial = jnp.dot(wcat[...], window, preferred_element_type=F32)
        result.append(silu_norm(spatial, half_two))
    return result


def tail_kernel(slots, groups, pack, ids, frame, pair, out, wcat, g1, g2, tails, *rest):
    sends, scr = rest[:-1], rest[-1]
    n, j = pl.program_id(0), pl.program_id(1)
    me, odd = ids[0], ids[1]
    rows = frame.shape[2]
    acts = act_rows(
        rows,
        lambda y: frame[0, 0, y].astype(F32),
        lambda: pair[0, 0].astype(F32),
        lambda: out[0, 0].astype(F32),
        wcat, g1, g2, scr, odd,
    )
    for y in range(rows):
        tails[0, 0, y] = acts[y]
    for s in range(1, groups):
        dst = lax.rem(me + s, groups)
        wanted = jnp.int32(-1)
        for k in range(slots):
            g = dst * slots + k
            hit = (pack[g, 0] > 0) & (pack[g, 2] == me)
            wanted = jnp.where(hit, pack[g, 3], wanted)

        @pl.when(wanted == n)
        def _():
            sends[s - 1][j] = tails[0, 0]


def main_kernel(slots, pack, ids, frame, pair, out, tails, wcat, wrot, g1, g2, result, heads, scr, ring):
    n, j = pl.program_id(0), pl.program_id(1)
    me, odd = ids[0], ids[1]
    frames, rows = pl.num_programs(1), frame.shape[2]
    chan = g1.shape[0]
    place = lax.rem(j, 3)
    base = pl.multiple_of(place * chan, 32)

    @pl.when(j < frames - TAIL)
    def _():
        acts = act_rows(
            rows,
            lambda y: frame[0, 0, y].astype(F32),
            lambda: pair[0, 0].astype(F32),
            lambda: out[0, 0].astype(F32),
            wcat, g1, g2, scr, odd,
        )
        for y in range(rows):
            ring[y, pl.ds(base, chan), :] = acts[y]

    @pl.when(j < TAIL)
    def _():
        for y in range(rows):
            heads[0, j, y] = ring[y, pl.ds(base, chan), :]

    @pl.when(j >= frames - TAIL)
    def _():
        for y in range(rows):
            ring[y, pl.ds(base, chan), :] = tails[0, 0, y]

    @pl.when(j >= TAIL)
    def _():
        keep = j < pack[me * slots + n, 1]
        for y in range(rows):
            temporal = jnp.dot(wrot[place], ring[y], preferred_element_type=F32)
            total = frame[0, 0, y].astype(F32) + temporal
            result[0, 0, y] = jnp.where(keep, total, 0.0).astype(BF16)


def head_kernel(slots, groups, pack, ids, frame, heads, tails, wtime, *rest):
    recvs, result, scr = rest[: groups - 1], rest[-2], rest[-1]
    n = pl.program_id(0)
    me = ids[0]
    rows, chan = frame.shape[2], frame.shape[3]
    g = me * slots + n
    has_prev, source = pack[g, 0] > 0, pack[g, 2]
    for y in range(rows):
        for f in range(TAIL):
            scr[y, (TAIL + f) * chan : (TAIL + f + 1) * chan, :] = heads[0, f, y]

    def put(load):
        for y in range(rows):
            for f in range(TAIL):
                scr[y, f * chan : (f + 1) * chan, :] = load(f, y)

    @pl.when(jnp.logical_not(has_prev))
    def _():
        put(lambda f, y: jnp.zeros(scr.shape[-1:], BF16) + jnp.zeros((chan, 1), BF16))

    @pl.when(has_prev & (source == me))
    def _():
        put(lambda f, y: tails[0, f, y])

    for s in range(1, groups):
        @pl.when(has_prev & (source == lax.rem(me + groups - s, groups)))
        def _():
            put(lambda f, y: recvs[s - 1][f, y])

    for f in range(TAIL):
        keep = f < pack[g, 1]
        for y in range(rows):
            window = scr[y, f * chan : (f + 3) * chan, :]
            temporal = jnp.dot(wtime[...], window, preferred_element_type=F32)
            total = frame[0, f, y].astype(F32) + temporal
            result[0, f, y] = jnp.where(keep, total, 0.0).astype(BF16)


def body(frames, packing, w_space, w_time, gain_one, gain_two):
    slots, count, rows, chan, cols = frames.shape
    groups, tiles = lax.axis_size("group"), lax.axis_size("tile")
    me = lax.axis_index("group").astype(jnp.int32)
    odd = lax.rem(lax.axis_index("tile"), 2).astype(jnp.int32)
    ids = jnp.stack([me, odd])
    lead = count - TAIL

    pairs = [(i, i ^ 1) for i in range(tiles)]
    outs = [(i, i + 1 if i % 2 else i - 1) for i in range(1, tiles - 1)]
    pair_row = (1 - odd) * (rows - 1)
    out_row = odd * (rows - 1)

    def edge(row, first, size):
        sizes = (slots, size, 1, chan, cols)
        return lax.dynamic_slice(frames, (0, first, row, 0, 0), sizes).reshape(slots, size, chan, cols)

    tail_pair = lax.ppermute(edge(pair_row, lead, TAIL), "tile", pairs)
    tail_out = lax.ppermute(edge(out_row, lead, TAIL), "tile", outs)
    lead_pair = lax.ppermute(edge(pair_row, 0, lead), "tile", pairs)
    lead_out = lax.ppermute(edge(out_row, 0, lead), "tile", outs)

    wcat = w_space.transpose(2, 0, 1, 3).reshape(chan, 9 * chan)
    wtime = w_time.transpose(1, 0, 2).reshape(chan, 3 * chan)
    wrot = jnp.stack(
        [
            jnp.concatenate([w_time[(slot - r + 2) % 3] for slot in range(3)], axis=1)
            for r in range(3)
        ]
    )
    half_one = jnp.broadcast_to((0.5 * gain_one)[:, None], (chan, cols))
    half_two = jnp.broadcast_to((0.5 * gain_two)[:, None], (chan, cols))

    row_block = (1, 1, rows, chan, cols)
    halo_block = (1, 1, chan, cols)
    whole = lambda shape: pl.BlockSpec(shape, lambda *_: (0,) * len(shape))
    frame_flops = 2 * rows * cols * chan * chan
    frame_bytes = 2 * rows * cols * chan

    tails, *sends = pl.pallas_call(
        functools.partial(tail_kernel, slots, groups),
        out_shape=[jax.ShapeDtypeStruct((slots, TAIL, rows, chan, cols), BF16)]
        + [jax.ShapeDtypeStruct((TAIL, rows, chan, cols), BF16)] * (groups - 1),
        grid_spec=pltpu.PrefetchScalarGridSpec(
            num_scalar_prefetch=2,
            grid=(slots, TAIL),
            in_specs=[
                pl.BlockSpec(row_block, lambda n, j, *_: (n, lead + j, 0, 0, 0)),
                pl.BlockSpec(halo_block, lambda n, j, *_: (n, j, 0, 0)),
                pl.BlockSpec(halo_block, lambda n, j, *_: (n, j, 0, 0)),
                whole((chan, 9 * chan)),
                whole((chan, cols)),
                whole((chan, cols)),
            ],
            out_specs=[pl.BlockSpec(row_block, lambda n, j, *_: (n, j, 0, 0, 0))]
            + [whole((TAIL, rows, chan, cols))] * (groups - 1),
            scratch_shapes=[pltpu.VMEM(((rows + 2) * 3 * chan, cols), BF16)],
        ),
        name="tails",
        cost_estimate=pl.CostEstimate(
            flops=slots * TAIL * 9 * frame_flops,
            bytes_accessed=slots * TAIL * 3 * frame_bytes,
            transcendentals=slots * TAIL * rows * cols * chan * 2,
        ),
    )(packing, ids, frames, tail_pair, tail_out, wcat, half_one, half_two)

    recvs = [
        lax.ppermute(sends[s - 1], "group", [(i, (i + s) % groups) for i in range(groups)])
        for s in range(1, groups)
    ]

    result, heads = pl.pallas_call(
        functools.partial(main_kernel, slots),
        out_shape=[
            jax.ShapeDtypeStruct(frames.shape, BF16),
            jax.ShapeDtypeStruct((slots, TAIL, rows, chan, cols), BF16),
        ],
        grid_spec=pltpu.PrefetchScalarGridSpec(
            num_scalar_prefetch=2,
            grid=(slots, count),
            in_specs=[
                pl.BlockSpec(row_block, lambda n, j, *_: (n, j, 0, 0, 0)),
                pl.BlockSpec(halo_block, lambda n, j, *_: (n, jnp.minimum(j, lead - 1), 0, 0)),
                pl.BlockSpec(halo_block, lambda n, j, *_: (n, jnp.minimum(j, lead - 1), 0, 0)),
                pl.BlockSpec(row_block, lambda n, j, *_: (n, jnp.maximum(j - lead, 0), 0, 0, 0)),
                whole((chan, 9 * chan)),
                whole((3, chan, 3 * chan)),
                whole((chan, cols)),
                whole((chan, cols)),
            ],
            out_specs=[
                pl.BlockSpec(row_block, lambda n, j, *_: (n, jnp.maximum(j, TAIL), 0, 0, 0)),
                pl.BlockSpec((1, TAIL, rows, chan, cols), lambda n, j, *_: (n, 0, 0, 0, 0)),
            ],
            scratch_shapes=[
                pltpu.VMEM(((rows + 2) * 3 * chan, cols), BF16),
                pltpu.VMEM((rows, 3 * chan, cols), BF16),
            ],
        ),
        name="lead",
        cost_estimate=pl.CostEstimate(
            flops=slots * lead * 12 * frame_flops,
            bytes_accessed=slots * count * 2 * frame_bytes,
            transcendentals=slots * lead * rows * cols * chan * 2,
        ),
    )(packing, ids, frames, lead_pair, lead_out, tails, wcat, wrot, half_one, half_two)

    head_block = (1, TAIL, rows, chan, cols)

    def local_tail(n, pack, ids):
        return (jnp.clip(pack[ids[0] * slots + n, 3], 0, slots - 1), 0, 0, 0, 0)

    return pl.pallas_call(
        functools.partial(head_kernel_entry, slots, groups),
        out_shape=jax.ShapeDtypeStruct(frames.shape, BF16),
        grid_spec=pltpu.PrefetchScalarGridSpec(
            num_scalar_prefetch=2,
            grid=(slots,),
            in_specs=[
                pl.BlockSpec(head_block, lambda n, *_: (n, 0, 0, 0, 0)),
                pl.BlockSpec(head_block, lambda n, *_: (n, 0, 0, 0, 0)),
                pl.BlockSpec(head_block, local_tail),
                whole((chan, 3 * chan)),
            ]
            + [whole((TAIL, rows, chan, cols))] * (groups - 1)
            + [pl.BlockSpec(memory_space=pl.ANY)],
            out_specs=pl.BlockSpec(head_block, lambda n, *_: (n, 0, 0, 0, 0)),
            scratch_shapes=[pltpu.VMEM((rows, 2 * TAIL * chan, cols), BF16)],
        ),
        input_output_aliases={6 + groups - 1: 0},
        name="heads",
        cost_estimate=pl.CostEstimate(
            flops=slots * TAIL * 3 * frame_flops,
            bytes_accessed=slots * TAIL * 4 * frame_bytes,
            transcendentals=0,
        ),
    )(packing, ids, frames, heads, tails, wtime, *recvs, result)


def head_kernel_entry(slots, groups, pack, ids, frame, heads, tails, wtime, *rest):
    recvs, result, scr = rest[: groups - 1], rest[-2], rest[-1]
    head_kernel(slots, groups, pack, ids, frame, heads, tails, wtime, *recvs, result, scr)


def solution(mesh):
    in_specs = (P("group", None, "tile", None, None), P(), P(), P(), P(), P())
    out_specs = P("group", None, "tile", None, None)
    return jax.shard_map(body, mesh=mesh, in_specs=in_specs, out_specs=out_specs, check_vma=False)
```

time: 205 us -> 64 us (0.31)
  matrix products: 101 us -> 0 us
  waiting for transfers between devices: 58.7 us -> 0.02 us
  Pallas kernels: 0 us -> 40.2 us
  other arithmetic: 21.8 us -> 1.55 us
  between operations: 13.6 us -> 0.21 us
  starting transfers between devices: 6.69 us -> 13.1 us
  local copies, waits for them, and re-layouts: 3.75 us -> 7.83 us
    dot_general x13 -> x0, matrix products: 101 us -> none  [the longest x9 72 us: body(): jnp.einsum('oi,nfyix->nfyox', w_space[tap_row, tap_col], window, preferre...]
    all_gather x1 -> x0, waiting for transfers between devices: 48.3 us -> none  [body(): piece = lax.all_gather(tails, 'group', axis=0, tiled=True)]
    pallas_call x0 -> x3, Pallas kernels: none -> 40.2 us  [the longest x1 26.1 us: body(): pl.pallas_call(functools.partial(main_kernel, slots), out_shape=[jax.Shap...]
    convert_element_type x2 -> x0, other arithmetic: 10.6 us -> none  [the longest x1 5.78 us: body(): act = norm_act(summed, gain_two).astype(jnp.bfloat16)]
    ppermute x2 -> x7, waiting for transfers between devices: 10.4 us -> 0.02 us  [the longest x3 0.01 us: body(): lax.ppermute(sends[s - 1], 'group', [(i, (i + s) % groups) for i in range...]
    concatenate x1 -> x0, other arithmetic: 7.08 us -> none  [extended_2(): block = jnp.concatenate([low, block, high], axis=dim)]
    ppermute x2 -> x7, starting transfers between devices: 6.68 us -> 13.1 us  [the longest x3 4.81 us: body(): lax.ppermute(sends[s - 1], 'group', [(i, (i + s) % groups) for i in range...]
    reshape x0 -> x4, local copies, waits for them, and re-layouts: none -> 4.31 us  [the longest x2 2.76 us: edge(): lax.dynamic_slice(frames, (0, first, row, 0, 0), sizes)]
  transfers between devices with their start and end apart: 3 -> 7, of which waited for: 3 -> 0; matrix products, arithmetic and copies ran while one was open for 6% -> 11% of each run, Pallas kernels for 0% -> 55%
where the time goes in v1:
time: 64 us; the launch traced here: 62.9 us
  Pallas kernels  40.2 us (63%)
  starting transfers between devices  13.1 us (20%)
  local copies, waits for them, and re-layouts  7.83 us (12%)
  other arithmetic  1.55 us (2%)
    pallas_call x1, Pallas kernels, body(): pl.pallas_call(functools.partial(main_kernel, slots), out_shape=[jax.Shap...  26.1 us
    pallas_call x1, Pallas kernels, body(): pl.pallas_call(functools.partial(tail_kernel, slots, groups), out_shape=[...  8.35 us
    pallas_call x1, Pallas kernels, body(): pl.pallas_call(functools.partial(head_kernel_entry, slots, groups), out_s...  5.71 us
    ppermute x3, starting transfers between devices, body(): lax.ppermute(sends[s - 1], 'group', [(i, (i + s) % groups) for i in range...  4.81 us
    ppermute x1, starting transfers between devices, body(): tail_out = lax.ppermute(edge(out_row, lead, TAIL), 'tile', outs)  4.58 us
    ppermute x1, starting transfers between devices, body(): lead_out = lax.ppermute(edge(out_row, 0, lead), 'tile', outs)  3.57 us
    reshape x2, local copies, waits for them, and re-layouts, edge(): lax.dynamic_slice(frames, (0, first, row, 0, 0), sizes)  2.76 us
    unnamed x22, local copies, waits for them, and re-layouts  1.82 us
  transfers between devices with their start and end apart: 7, of which 0 were waited for; matrix products, arithmetic and copies ran while one was open for 11% of the time, Pallas kernels for 55%

profile of v1, /device:TPU:1, one launch (start us, length us, event | category | flops | bytes accessed | tf_op | source)
XLA Modules:
  0.0 62.9 jit_solution(7662323764453777781)
XLA Ops:
  0.0 1.2 %dynamic-slice_bitcast_fusion.2 = (bf16[3,2,96,256]{3,2,1,0:T(8,128)(2,1)S(1)}, bf16[3,2,96,256]{3,2,1,0:T(8,128)(2,1)S(1)}) fusion(bf16[3,8,4,96,256]{4,3,2,1,0:T(8,128)(2,1)} %frame.5, s32[]{:T(128)S(6)} %select_n.9, s32[]{:T(128)S(6)} %select_n.8), kind=kLoop, calls=%fused_computation.2 | loop fusion | bytes 1179656 | tf_op jit(solution)/shard_map/reshape | solution.py:170
  1.2 4.6 %collective-permute-start.3 = (bf16[3,2,96,256]{3,2,1,0:T(8,128)(2,1)S(1)}, bf16[3,2,96,256]{3,2,1,0:T(8,128)(2,1)S(1)}, u32[]{:S(2)}, u32[]{:S(2)}) collective-permute-start(bf16[3,2,96,256]{3,2,1,0:T(8,128)(2,1)S(1)} %get-tuple-element.17), channel_id=1, source_target_pairs={{1,2},{2,1},{3,4},{4,3},{5,6},{6,5},{7,8},{8,7},{9,10},{10,9},{11,... | collective-permute-start | bytes 884744 | tf_op jit(solution)/shard_map/ppermute | solution.py:173
  5.8 0.1 collective-permute-start.2
  5.9 1.6 %dynamic-slice_bitcast_fusion = (bf16[3,6,96,256]{3,2,1,0:T(8,128)(2,1)S(1)}, bf16[3,6,96,256]{3,2,1,0:T(8,128)(2,1)S(1)}) fusion(bf16[3,8,4,96,256]{4,3,2,1,0:T(8,128)(2,1)} %frame.5, s32[]{:T(128)S(6)} %select_n.9, s32[]{:T(128)S(6)} %select_n.8), kind=kLoop, calls=%fused_computation | loop fusion | bytes 3538952 | tf_op jit(solution)/shard_map/reshape | solution.py:170
  7.5 3.6 %collective-permute-start.1 = (bf16[3,6,96,256]{3,2,1,0:T(8,128)(2,1)S(1)}, bf16[3,6,96,256]{3,2,1,0:T(8,128)(2,1)}, u32[]{:S(2)}, u32[]{:S(2)}) collective-permute-start(bf16[3,6,96,256]{3,2,1,0:T(8,128)(2,1)S(1)} %get-tuple-element.19), channel_id=1, source_target_pairs={{1,2},{2,1},{3,4},{4,3},{5,6},{6,5},{7,8},{8,7},{9,10},{10,9},{11,... | collective-permute-start | bytes 2654216 | tf_op jit(solution)/shard_map/ppermute | solution.py:175
  11.1 0.1 collective-permute-start
  11.2 0.7 %copy.19.pack = s32[12,4]{1,0:T(8,128)} copy(s32[12,4]{0,1:T(4,128)S(1)} %copy-done.7) | data formatting | bytes 384 | tf_op args[1]
  11.9 0.2 copy.13
  12.1 0.8 %copy.15.wcat = bf16[96,864]{1,0:T(8,128)(2,1)} copy(bf16[96,864]{0,1:T(8,128)(2,1)S(1)} %bitcast.27) | data formatting | bytes 331776 | tf_op jit(solution)/shard_map/reshape | solution.py:177
  12.9 0.1 maximum_bitcast_fusion
  13.1 0.6 %pad_add_fusion.ids = s32[2]{0:T(128)} fusion(s32[1]{0:T(128)} %bitcast.1, s32[1]{0:T(128)} %bitcast), kind=kLoop, calls=%fused_computation.11 | loop fusion | flops 2 | bytes 16 | tf_op jit(solution)/shard_map/stack | solution.py:160
  13.7 0.0 collective-permute-done.3.out
  13.7 0.0 collective-permute-done.2.pair
  13.8 0.0 copy-start.4
  13.8 0.8 %broadcast_in_dim.5.g2 = f32[96,256]{1,0:T(8,128)} broadcast(f32[96]{0:T(128)S(1)} %broadcast_multiply_fusion), dimensions={0} | broadcast | bytes 98688 | tf_op jit(solution)/shard_map/broadcast_in_dim | solution.py:186
  14.6 0.7 %broadcast_in_dim.4.g1 = f32[96,256]{1,0:T(8,128)} broadcast(f32[96]{0:T(128)S(1)} %broadcast_multiply_fusion.1), dimensions={0} | broadcast | bytes 98688 | tf_op jit(solution)/shard_map/broadcast_in_dim | solution.py:185
  15.3 8.3 %tails.1 = (bf16[3,2,4,96,256]{4,3,2,1,0:T(8,128)(2,1)}, bf16[2,4,96,256]{3,2,1,0:T(8,128)(2,1)}, bf16[2,4,96,256]{3,2,1,0:T(8,128)(2,1)}, bf16[2,4,96,256]{3,2,1,0:T(8,128)(2,1)}) custom-call(s32[12,4]{1,0:T(8,128)} %copy.19.pack, s32[2]{0:T(128)} %pad_add_fusion.ids, bf16[3,8,4,96,256]{4,3,2,1,0:T(8,128)(2,1)} %frame.5, bf16[3,2,96,256]{3,2,1,0:T(8,128)(2,1)} %copy-done.4, ...), custom_call_target="tpu_custom_call" | custom-call | flops 1019215872 | bytes 3538944 | tf_op jit(solution)/shard_map/tails/pallas_call | solution.py:194
  23.6 1.2 %collective-permute-start.4 = (bf16[2,4,96,256]{3,2,1,0:T(8,128)(2,1)}, bf16[2,4,96,256]{3,2,1,0:T(8,128)(2,1)S(1)}, u32[]{:S(2)}, u32[]{:S(2)}) collective-permute-start(bf16[2,4,96,256]{3,2,1,0:T(8,128)(2,1)} %get-tuple-element.13), channel_id=1, source_target_pairs={{0,32},{32,64},{64,96},{96,0},{1,33},{33,65},{65,97},{97,1},{2,34}... | collective-permute-start | bytes 1179656 | tf_op jit(solution)/shard_map/ppermute | solution.py:222
  24.8 2.5 %collective-permute-start.5 = (bf16[2,4,96,256]{3,2,1,0:T(8,128)(2,1)}, bf16[2,4,96,256]{3,2,1,0:T(8,128)(2,1)S(1)}, u32[]{:S(2)}, u32[]{:S(2)}) collective-permute-start(bf16[2,4,96,256]{3,2,1,0:T(8,128)(2,1)} %get-tuple-element.14), channel_id=1, source_target_pairs={{0,64},{32,96},{64,0},{96,32},{1,65},{33,97},{65,1},{97,33},{2,66}... | collective-permute-start | bytes 1179656 | tf_op jit(solution)/shard_map/ppermute | solution.py:222
  27.3 1.1 %collective-permute-start.6 = (bf16[2,4,96,256]{3,2,1,0:T(8,128)(2,1)}, bf16[2,4,96,256]{3,2,1,0:T(8,128)(2,1)S(1)}, u32[]{:S(2)}, u32[]{:S(2)}) collective-permute-start(bf16[2,4,96,256]{3,2,1,0:T(8,128)(2,1)} %get-tuple-element.15), channel_id=1, source_target_pairs={{0,96},{32,0},{64,32},{96,64},{1,97},{33,1},{65,33},{97,65},{2,98}... | collective-permute-start | bytes 1179656 | tf_op jit(solution)/shard_map/ppermute | solution.py:222
  28.4 0.7 %pad_maximum_fusion.wrot = bf16[3,96,288]{2,1,0:T(8,128)(2,1)} fusion(bf16[1,96,288]{2,1,0:T(8,128)(2,1)S(1)} %get-tuple-element.22, bf16[1,96,288]{2,1,0:T(8,128)(2,1)S(1)} %get-tuple-element.23, bf16[1,96,288]{2,1,0:T(8,128)(2,1)S(1)} %get-tuple-element.21), kind=kLoop, calls=%fused_computation.4 | loop fusion | flops 165888 | bytes 331776 | tf_op jit(solution)/shard_map/stack | solution.py:179
  29.2 0.1 copy.18
  29.3 0.7 %copy.20.wtime = bf16[96,288]{1,0:T(8,128)(2,1)} copy(bf16[96,288]{0,1:T(8,128)(2,1)S(1)} %bitcast.28) | data formatting | bytes 110592 | tf_op jit(solution)/shard_map/reshape | solution.py:178
  30.0 0.0 collective-permute-done.1.out
  30.0 0.0 collective-permute-done.pair
  30.0 26.1 %lead.1 = (bf16[3,8,4,96,256]{4,3,2,1,0:T(8,128)(2,1)}, bf16[3,2,4,96,256]{4,3,2,1,0:T(8,128)(2,1)}) custom-call(s32[12,4]{1,0:T(8,128)} %copy.19.pack, s32[2]{0:T(128)} %pad_add_fusion.ids, bf16[3,8,4,96,256]{4,3,2,1,0:T(8,128)(2,1)} %frame.5, bf16[3,6,96,256]{3,2,1,0:T(8,128)(2,1)} %collective-permute-done.pair, ...), custom_call_target="tpu_custom_call" | custom-call | flops 4076863488 | bytes 9437184 | tf_op jit(solution)/shard_map/lead/pallas_call | solution.py:226
  56.1 0.0 collective-permute-done.5.rest_1_
  56.2 0.0 collective-permute-done.6.rest_2_
  56.2 0.7 %copy-done = bf16[2,4,96,256]{3,2,1,0:T(8,128)(2,1)} copy-done((bf16[2,4,96,256]{3,2,1,0:T(8,128)(2,1)}, bf16[2,4,96,256]{3,2,1,0:T(8,128)(2,1)S(1)}, u32[]{:S(2)}) %copy-start) | copy-done | bytes 393240
  56.9 0.1 copy-done.1
  57.0 0.1 copy-done.2
  57.2 5.7 %heads.1 = bf16[3,8,4,96,256]{4,3,2,1,0:T(8,128)(2,1)} custom-call(s32[12,4]{1,0:T(8,128)} %copy.19.pack, s32[2]{0:T(128)} %pad_add_fusion.ids, bf16[3,8,4,96,256]{4,3,2,1,0:T(8,128)(2,1)} %frame.5, bf16[3,2,4,96,256]{4,3,2,1,0:T(8,128)(2,1)} %get-tuple-element.12.heads, ...), custom_call_target="tpu_custom_call", output_to_operand_aliasing={{}: (9, {})} | custom-call | flops 339738624 | bytes 4718592 | tf_op jit(solution)/shard_map/heads/pallas_call | solution.py:267
  (20 shorter events, 0.0 us)
Async XLA Ops:
  0.0 11.2 %copy-start.7 = (s32[12,4]{0,1:T(4,128)S(1)}, s32[12,4]{0,1:T(4,128)}, u32[]{:S(2)}) copy-start(s32[12,4]{0,1:T(4,128)} %param.7) | copy-start | bytes 580
  0.0 11.9 %copy-start.5 = (bf16[3,96,96]{2,1,0:T(8,128)(2,1)S(1)}, bf16[3,96,96]{2,1,0:T(8,128)(2,1)}, u32[]{:S(2)}) copy-start(bf16[3,96,96]{2,1,0:T(8,128)(2,1)} %param.9) | copy-start | bytes 165892
  0.0 11.9 %copy-start.6 = (bf16[3,3,96,96]{3,2,1,0:T(8,128)(2,1)S(1)}, bf16[3,3,96,96]{3,2,1,0:T(8,128)(2,1)}, u32[]{:S(2)}) copy-start(bf16[3,3,96,96]{3,2,1,0:T(8,128)(2,1)} %param.8) | copy-start | bytes 497668
  0.0 13.0 %copy-start.8 = (f32[96]{0:T(128)S(1)}, f32[96]{0:T(128)}, u32[]{:S(2)}) copy-start(f32[96]{0:T(128)} %param.10) | copy-start | bytes 1156
  0.0 13.7 %copy-start.9 = (f32[96]{0:T(128)S(1)}, f32[96]{0:T(128)}, u32[]{:S(2)}) copy-start(f32[96]{0:T(128)} %param.11) | copy-start | bytes 1156
  1.2 12.5 %collective-permute-start.3 = (bf16[3,2,96,256]{3,2,1,0:T(8,128)(2,1)S(1)}, bf16[3,2,96,256]{3,2,1,0:T(8,128)(2,1)S(1)}, u32[]{:S(2)}, u32[]{:S(2)}) collective-permute-start(bf16[3,2,96,256]{3,2,1,0:T(8,128)(2,1)S(1)} %get-tuple-element.17), channel_id=1, source_target_pairs={{1,2},{2,1},{3,4},{4,3},{5,6},{6,5},{7,8},{8,7},{9,10},{10,9},{11,... | collective-permute-start | bytes 884744 | tf_op jit(solution)/shard_map/ppermute | solution.py:173
  5.8 7.9 %collective-permute-start.2 = (bf16[3,2,96,256]{3,2,1,0:T(8,128)(2,1)S(1)}, bf16[3,2,96,256]{3,2,1,0:T(8,128)(2,1)S(1)}, u32[]{:S(2)}, u32[]{:S(2)}) collective-permute-start(bf16[3,2,96,256]{3,2,1,0:T(8,128)(2,1)S(1)} %get-tuple-element.18), channel_id=1, source_target_pairs={{0,1},{1,0},{2,3},{3,2},{4,5},{5,4},{6,7},{7,6},{8,9},{9,8},{10,11... | collective-permute-start | bytes 884744 | tf_op jit(solution)/shard_map/ppermute | solution.py:172
  7.5 22.5 %collective-permute-start.1 = (bf16[3,6,96,256]{3,2,1,0:T(8,128)(2,1)S(1)}, bf16[3,6,96,256]{3,2,1,0:T(8,128)(2,1)}, u32[]{:S(2)}, u32[]{:S(2)}) collective-permute-start(bf16[3,6,96,256]{3,2,1,0:T(8,128)(2,1)S(1)} %get-tuple-element.19), channel_id=1, source_target_pairs={{1,2},{2,1},{3,4},{4,3},{5,6},{6,5},{7,8},{8,7},{9,10},{10,9},{11,... | collective-permute-start | bytes 2654216 | tf_op jit(solution)/shard_map/ppermute | solution.py:175
  11.1 19.0 %collective-permute-start = (bf16[3,6,96,256]{3,2,1,0:T(8,128)(2,1)S(1)}, bf16[3,6,96,256]{3,2,1,0:T(8,128)(2,1)}, u32[]{:S(2)}, u32[]{:S(2)}) collective-permute-start(bf16[3,6,96,256]{3,2,1,0:T(8,128)(2,1)S(1)} %get-tuple-element.20), channel_id=1, source_target_pairs={{0,1},{1,0},{2,3},{3,2},{4,5},{5,4},{6,7},{7,6},{8,9},{9,8},{10,11... | collective-permute-start | bytes 2654216 | tf_op jit(solution)/shard_map/ppermute | solution.py:174
  13.7 1.5 %copy-start.3 = (bf16[3,2,96,256]{3,2,1,0:T(8,128)(2,1)}, bf16[3,2,96,256]{3,2,1,0:T(8,128)(2,1)S(1)}, u32[]{:S(2)}) copy-start(bf16[3,2,96,256]{3,2,1,0:T(8,128)(2,1)S(1)} %collective-permute-done.3.out) | copy-start | bytes 884740
  13.8 1.5 %copy-start.4 = (bf16[3,2,96,256]{3,2,1,0:T(8,128)(2,1)}, bf16[3,2,96,256]{3,2,1,0:T(8,128)(2,1)S(1)}, u32[]{:S(2)}) copy-start(bf16[3,2,96,256]{3,2,1,0:T(8,128)(2,1)S(1)} %collective-permute-done.2.pair) | copy-start | bytes 884740
  23.6 32.5 %collective-permute-start.4 = (bf16[2,4,96,256]{3,2,1,0:T(8,128)(2,1)}, bf16[2,4,96,256]{3,2,1,0:T(8,128)(2,1)S(1)}, u32[]{:S(2)}, u32[]{:S(2)}) collective-permute-start(bf16[2,4,96,256]{3,2,1,0:T(8,128)(2,1)} %get-tuple-element.13), channel_id=1, source_target_pairs={{0,32},{32,64},{64,96},{96,0},{1,33},{33,65},{65,97},{97,1},{2,34}... | collective-permute-start | bytes 1179656 | tf_op jit(solution)/shard_map/ppermute | solution.py:222
  24.8 31.3 %collective-permute-start.5 = (bf16[2,4,96,256]{3,2,1,0:T(8,128)(2,1)}, bf16[2,4,96,256]{3,2,1,0:T(8,128)(2,1)S(1)}, u32[]{:S(2)}, u32[]{:S(2)}) collective-permute-start(bf16[2,4,96,256]{3,2,1,0:T(8,128)(2,1)} %get-tuple-element.14), channel_id=1, source_target_pairs={{0,64},{32,96},{64,0},{96,32},{1,65},{33,97},{65,1},{97,33},{2,66}... | collective-permute-start | bytes 1179656 | tf_op jit(solution)/shard_map/ppermute | solution.py:222
  27.3 28.9 %collective-permute-start.6 = (bf16[2,4,96,256]{3,2,1,0:T(8,128)(2,1)}, bf16[2,4,96,256]{3,2,1,0:T(8,128)(2,1)S(1)}, u32[]{:S(2)}, u32[]{:S(2)}) collective-permute-start(bf16[2,4,96,256]{3,2,1,0:T(8,128)(2,1)} %get-tuple-element.15), channel_id=1, source_target_pairs={{0,96},{32,0},{64,32},{96,64},{1,97},{33,1},{65,33},{97,65},{2,98}... | collective-permute-start | bytes 1179656 | tf_op jit(solution)/shard_map/ppermute | solution.py:222
  56.1 0.8 %copy-start = (bf16[2,4,96,256]{3,2,1,0:T(8,128)(2,1)}, bf16[2,4,96,256]{3,2,1,0:T(8,128)(2,1)S(1)}, u32[]{:S(2)}) copy-start(bf16[2,4,96,256]{3,2,1,0:T(8,128)(2,1)S(1)} %collective-permute-done.4.rest_0_) | copy-start | bytes 1179652
  56.2 0.9 %copy-start.1 = (bf16[2,4,96,256]{3,2,1,0:T(8,128)(2,1)}, bf16[2,4,96,256]{3,2,1,0:T(8,128)(2,1)S(1)}, u32[]{:S(2)}) copy-start(bf16[2,4,96,256]{3,2,1,0:T(8,128)(2,1)S(1)} %collective-permute-done.5.rest_1_) | copy-start | bytes 1179652
  56.2 1.0 %copy-start.2 = (bf16[2,4,96,256]{3,2,1,0:T(8,128)(2,1)}, bf16[2,4,96,256]{3,2,1,0:T(8,128)(2,1)S(1)}, u32[]{:S(2)}) copy-start(bf16[2,4,96,256]{3,2,1,0:T(8,128)(2,1)S(1)} %collective-permute-done.6.rest_2_) | copy-start | bytes 1179652
